TPU v7x, 32 devices: a whole 2x2x4 slice. The times are simulated.
32 devices in a mesh: batch: 8 (over z, core), seq: 4 (over y, x).
Axes of the slice: x: 2, y: 2, z: 4, core: 2. Of those that a mesh axis runs over, the one named last changes fastest.
Arguments:
- tokens: bfloat16 [16, 1024, 1152], P('batch', 'seq')
- prefix_len: int32 [16], P('batch'), may hold values from 102 to 512
- attention_gain: float32 [1152], replicated, may hold values from 0.1 to 1.9
- query_weight: bfloat16 [1152, 1152], P('batch', 'seq'), may hold values from -0.1875 to 0.1875
- key_weight: bfloat16 [1152, 384], P('batch', 'seq'), may hold values from -0.1875 to 0.1875
- value_weight: bfloat16 [1152, 384], P('batch', 'seq'), may hold values from -0.1875 to 0.1875
- output_weight: bfloat16 [1152, 1152], P('batch', 'seq'), may hold values from -4 to 4
- mlp_gain: float32 [1152], replicated, may hold values from 0.1 to 1.9
- gate_weight: bfloat16 [1152, 3072], P('batch', 'seq'), may hold values from -0.1875 to 0.1875
- up_weight: bfloat16 [1152, 3072], P('batch', 'seq'), may hold values from -0.1875 to 0.1875
- down_weight: bfloat16 [3072, 1152], P('batch', 'seq'), may hold values from -0.109375 to 0.109375
- cotangent: bfloat16 [16, 1024, 1152], P('batch', 'seq'), may hold values from -6 to 6
Outputs:
- layer_output: bfloat16 [16, 1024, 1152], P('batch', 'seq')
- input_grad: float32 [16, 1024, 1152], P('batch', 'seq')
- attention_gain_grad: float32 [1152], replicated
- query_grad: float32 [1152, 1152], P('batch', 'seq')
- key_grad: float32 [1152, 384], P('batch', 'seq')
- value_grad: float32 [1152, 384], P('batch', 'seq')
- output_grad: float32 [1152, 1152], P('batch', 'seq')
- mlp_gain_grad: float32 [1152], replicated
- gate_grad: float32 [1152, 3072], P('batch', 'seq')
- up_grad: float32 [1152, 3072], P('batch', 'seq')
- down_weight_gradient: float32 [3072, 1152], P('batch', 'seq')
- residual_rms: float32 [3], replicated
All inputs are finite; a program needn't handle non-finite values.
Results may differ from a plain program's by a relative error of at most 0.02.
Values may be sent and summed in bfloat16 or wider, within the bound.
No kernel may reach another device: no remote copies, remote signals or barrier semaphores. Data moves between devices by JAX's collectives and lax.ppermute only.
A program may use at most 192 MiB of HBM per device.

v0:
```python
import jax
import jax.numpy as jnp
from jax import lax
from jax.sharding import PartitionSpec as P

HEADS = 18
KV_HEADS = 6
HEAD = 64
SEQ_LEN = 1024
EPSILON = 1e-05
MASKED = -1e30


def rope_tables(positions, half_width):
    frequency = 10000.0 ** (-(jnp.arange(half_width, dtype=jnp.float32) * 2.0) / (2.0 * half_width))
    angles = positions.astype(jnp.float32)[:, None] * frequency[None, :]
    return (jnp.cos(angles)[:, None, :], jnp.sin(angles)[:, None, :])


def rotate(values, cosine, sine):
    half_width = values.shape[-1] // 2
    former = values[..., :half_width]
    trailing_operand = values[..., half_width:]
    return jnp.concatenate(
        [former * cosine - trailing_operand * sine, trailing_operand * cosine + former * sine], -1
    )


def unrotate(values, cosine, sine):
    half_width = values.shape[-1] // 2
    former = values[..., :half_width]
    trailing_operand = values[..., half_width:]
    return jnp.concatenate(
        [former * cosine + trailing_operand * sine, trailing_operand * cosine - former * sine], -1
    )


def gather_weights(weights):
    rows = (
        lax.all_gather(weights[0], "batch", axis=0, tiled=True),
        lax.all_gather(weights[1], "batch", axis=0, tiled=True),
        lax.all_gather(weights[2], "batch", axis=0, tiled=True),
        lax.all_gather(weights[3], "batch", axis=0, tiled=True),
        lax.all_gather(weights[4], "batch", axis=0, tiled=True),
        lax.all_gather(weights[5], "batch", axis=0, tiled=True),
        lax.all_gather(weights[6], "batch", axis=0, tiled=True),
    )
    return (
        lax.all_gather(rows[0], "seq", axis=1, tiled=True),
        lax.all_gather(rows[1], "seq", axis=1, tiled=True),
        lax.all_gather(rows[2], "seq", axis=1, tiled=True),
        lax.all_gather(rows[3], "seq", axis=1, tiled=True),
        lax.all_gather(rows[4], "seq", axis=1, tiled=True),
        lax.all_gather(rows[5], "seq", axis=1, tiled=True),
        lax.all_gather(rows[6], "seq", axis=1, tiled=True),
    )


def to_query_heads(values):
    seqs_here, local_len = (values.shape[0], values.shape[1])
    shaped = values.reshape(seqs_here, local_len, KV_HEADS, HEADS // KV_HEADS, HEAD)
    return shaped.transpose(2, 0, 3, 1, 4)


def from_query_heads(values):
    seqs_here, local_len = (values.shape[1], values.shape[3])
    return values.transpose(1, 3, 0, 2, 4).reshape(seqs_here, local_len, HEADS * HEAD)


def to_kv_heads(values):
    seqs_here, length = (values.shape[0], values.shape[1])
    return values.reshape(seqs_here, length, KV_HEADS, HEAD).transpose(2, 0, 1, 3)


def from_kv_heads(values):
    seqs_here, length = (values.shape[1], values.shape[2])
    return values.transpose(1, 2, 0, 3).reshape(seqs_here, length, KV_HEADS * HEAD)


def head_scores(query_group, key_group, visible):
    scores = jnp.einsum(
        "sgld,skd->sglk", query_group, key_group, preferred_element_type=jnp.float32
    ) * HEAD ** (-0.5)
    return jnp.where(visible[:, None], scores, MASKED)


def attend(query_group, key_group, value_group, visible):
    scores = head_scores(query_group, key_group, visible)
    highest = jnp.max(scores, -1, keepdims=True)
    expo = jnp.exp(scores - highest)
    totals = jnp.sum(expo, -1, keepdims=True)
    weights = (expo / totals).astype(jnp.bfloat16)
    mixed = jnp.einsum("sglk,skd->sgld", weights, value_group, preferred_element_type=jnp.float32)
    return (mixed, (highest + jnp.log(totals))[..., 0])


def attend_back(query_group, key_group, value_group, log_total, d_mixed, visible):
    scores = head_scores(query_group, key_group, visible)
    weights = jnp.exp(scores - log_total[..., None])
    low_weights = weights.astype(jnp.bfloat16)
    d_weights = jnp.einsum(
        "sgld,skd->sglk", d_mixed, value_group, preferred_element_type=jnp.float32
    )
    d_scores = weights * (d_weights - jnp.sum(weights * d_weights, -1, keepdims=True))
    low_scores = d_scores.astype(jnp.bfloat16)
    scale = HEAD ** (-0.5)
    d_query = (
        jnp.einsum("sglk,skd->sgld", low_scores, key_group, preferred_element_type=jnp.float32)
        * scale
    )
    d_key = (
        jnp.einsum("sglk,sgld->skd", low_scores, query_group, preferred_element_type=jnp.float32)
        * scale
    )
    d_value = jnp.einsum("sglk,sgld->skd", low_weights, d_mixed, preferred_element_type=jnp.float32)
    return (d_query, d_key, d_value)


def norm_back(upstream, inputs, inverse, gain):
    scaled = upstream * gain
    inner = jnp.sum(scaled * inputs, -1, keepdims=True)
    d_inputs = inverse * scaled - inputs * inverse * inverse * inverse * inner / inputs.shape[-1]
    return (d_inputs, jnp.sum(upstream * inputs * inverse, (0, 1)))


def apply_projection(left_operand, right_operand):
    return jnp.einsum(
        "jnh,hb->jnb", left_operand, right_operand, preferred_element_type=jnp.float32
    )


def project_back(left_operand, right_operand):
    return jnp.einsum(
        "vui,ri->vur", left_operand, right_operand, preferred_element_type=jnp.float32
    )


def weight_grad(left_operand, right_operand):
    return jnp.einsum(
        "nzt,nzq->tq", left_operand, right_operand, preferred_element_type=jnp.float32
    )


def on_device(
    tokens,
    prefix_len,
    attention_gain,
    query_weight,
    key_weight,
    value_weight,
    output_weight,
    mlp_gain,
    gate_weight,
    up_weight,
    down_weight,
    cotangent,
):
    seqs_here, local_len, width = tokens.shape
    offset = lax.axis_index("seq") * local_len
    row_position = offset + jnp.arange(local_len, dtype=jnp.int32)
    key_position = jnp.arange(SEQ_LEN, dtype=jnp.int32)
    visible = (key_position[None, None, :] <= row_position[None, :, None]) | (
        key_position[None, None, :] < prefix_len[:, None, None]
    )
    cosine, sine = rope_tables(row_position, HEAD // 2)
    shards = (
        query_weight,
        key_weight,
        value_weight,
        output_weight,
        gate_weight,
        up_weight,
        down_weight,
    )
    gathered = gather_weights(shards)
    w_query, w_key, w_value, w_output, w_gate, w_up, w_down = gathered
    inputs = tokens.astype(jnp.float32)
    inverse_a = lax.rsqrt(jnp.mean(inputs * inputs, -1, keepdims=True) + EPSILON)
    normed_a = (inputs * inverse_a * attention_gain).astype(jnp.bfloat16)
    query_pre = apply_projection(normed_a, w_query)
    key_pre = apply_projection(normed_a, w_key)
    value_low = apply_projection(normed_a, w_value).astype(jnp.bfloat16)
    query_rot = rotate(query_pre.reshape(seqs_here, local_len, HEADS, HEAD), cosine, sine).astype(
        jnp.bfloat16
    )
    key_rot = rotate(key_pre.reshape(seqs_here, local_len, KV_HEADS, HEAD), cosine, sine).astype(
        jnp.bfloat16
    )
    key_rot = key_rot.reshape(seqs_here, local_len, KV_HEADS * HEAD)
    gathered_key_rows, value_all = (
        lax.all_gather(key_rot, "seq", axis=1, tiled=True),
        lax.all_gather(value_low, "seq", axis=1, tiled=True),
    )
    query_heads = to_query_heads(query_rot)
    key_heads = to_kv_heads(gathered_key_rows)
    value_heads = to_kv_heads(value_all)

    def forward_head(packed):
        return attend(packed[0], packed[1], packed[2], visible)

    mixed_heads, log_totals = lax.map(forward_head, (query_heads, key_heads, value_heads))
    mixed = from_query_heads(mixed_heads).astype(jnp.bfloat16)
    attn_branch = apply_projection(mixed, w_output)
    middle = inputs + attn_branch
    inverse_m = lax.rsqrt(jnp.mean(middle * middle, -1, keepdims=True) + EPSILON)
    normed_m = (middle * inverse_m * mlp_gain).astype(jnp.bfloat16)
    gate_pre = apply_projection(normed_m, w_gate)
    upper_pre = apply_projection(normed_m, w_up)
    sigmoid_gate = jax.nn.sigmoid(gate_pre)
    silu_gate = gate_pre * sigmoid_gate
    hidden = (silu_gate * upper_pre).astype(jnp.bfloat16)
    mlp_branch = apply_projection(hidden, w_down)
    layer_output = (middle + mlp_branch).astype(jnp.bfloat16)
    held = lax.optimization_barrier((shards, cotangent))
    again = gather_weights(held[0])
    query_back, key_back, value_back, output_back, gate_back, up_back, down_back = again
    upstream = cotangent.astype(jnp.float32)
    d_mlp = upstream.astype(jnp.bfloat16)
    grad_down = weight_grad(hidden, d_mlp)
    d_hidden = project_back(d_mlp, down_back)
    d_gate = (d_hidden * upper_pre * sigmoid_gate * (1.0 + gate_pre * (1.0 - sigmoid_gate))).astype(
        jnp.bfloat16
    )
    d_upper = (d_hidden * silu_gate).astype(jnp.bfloat16)
    grad_gate = weight_grad(normed_m, d_gate)
    upper_half_gradient = weight_grad(normed_m, d_upper)
    d_normed_m = project_back(d_gate, gate_back) + project_back(d_upper, up_back)
    d_middle_norm, gain_m_part = norm_back(d_normed_m, middle, inverse_m, mlp_gain)
    d_middle = upstream + d_middle_norm
    d_attn = d_middle.astype(jnp.bfloat16)
    grad_output = weight_grad(mixed, d_attn)
    d_mixed = project_back(d_attn, output_back).astype(jnp.bfloat16)

    def backward_head(packed):
        return attend_back(packed[0], packed[1], packed[2], packed[3], packed[4], visible)

    dq_heads, dk_heads, dv_heads = lax.map(
        backward_head, (query_heads, key_heads, value_heads, log_totals, to_query_heads(d_mixed))
    )
    key_grad_all = from_kv_heads(dk_heads)
    value_grad_all = from_kv_heads(dv_heads)
    key_grad_mine, value_grad_mine = (
        lax.psum_scatter(
            key_grad_all.astype(jnp.bfloat16), "seq", scatter_dimension=1, tiled=True
        ).astype(jnp.float32),
        lax.psum_scatter(
            value_grad_all.astype(jnp.bfloat16), "seq", scatter_dimension=1, tiled=True
        ).astype(jnp.float32),
    )
    d_query_rot = from_query_heads(dq_heads).reshape(seqs_here, local_len, HEADS, HEAD)
    d_query = (
        unrotate(d_query_rot, cosine, sine)
        .reshape(seqs_here, local_len, HEADS * HEAD)
        .astype(jnp.bfloat16)
    )
    d_key = unrotate(key_grad_mine.reshape(seqs_here, local_len, KV_HEADS, HEAD), cosine, sine)
    d_key = d_key.reshape(seqs_here, local_len, KV_HEADS * HEAD).astype(jnp.bfloat16)
    d_value = value_grad_mine.astype(jnp.bfloat16)
    grad_query = weight_grad(normed_a, d_query)
    grad_key = weight_grad(normed_a, d_key)
    value_gradient_rows = weight_grad(normed_a, d_value)
    d_normed_a = (
        project_back(d_query, query_back)
        + project_back(d_key, key_back)
        + project_back(d_value, value_back)
    )
    d_inputs_norm, gain_a_part = norm_back(d_normed_a, inputs, inverse_a, attention_gain)
    input_grad = d_middle + d_inputs_norm
    columns = (
        lax.psum_scatter(
            grad_query.astype(jnp.bfloat16), "seq", scatter_dimension=1, tiled=True
        ).astype(jnp.float32),
        lax.psum_scatter(
            grad_key.astype(jnp.bfloat16), "seq", scatter_dimension=1, tiled=True
        ).astype(jnp.float32),
        lax.psum_scatter(
            value_gradient_rows.astype(jnp.bfloat16), "seq", scatter_dimension=1, tiled=True
        ).astype(jnp.float32),
        lax.psum_scatter(
            grad_output.astype(jnp.bfloat16), "seq", scatter_dimension=1, tiled=True
        ).astype(jnp.float32),
        lax.psum_scatter(
            grad_gate.astype(jnp.bfloat16), "seq", scatter_dimension=1, tiled=True
        ).astype(jnp.float32),
        lax.psum_scatter(
            upper_half_gradient.astype(jnp.bfloat16), "seq", scatter_dimension=1, tiled=True
        ).astype(jnp.float32),
        lax.psum_scatter(
            grad_down.astype(jnp.bfloat16), "seq", scatter_dimension=1, tiled=True
        ).astype(jnp.float32),
    )
    owned = (
        lax.psum_scatter(
            columns[0].astype(jnp.bfloat16), "batch", scatter_dimension=0, tiled=True
        ).astype(jnp.float32),
        lax.psum_scatter(
            columns[1].astype(jnp.bfloat16), "batch", scatter_dimension=0, tiled=True
        ).astype(jnp.float32),
        lax.psum_scatter(
            columns[2].astype(jnp.bfloat16), "batch", scatter_dimension=0, tiled=True
        ).astype(jnp.float32),
        lax.psum_scatter(
            columns[3].astype(jnp.bfloat16), "batch", scatter_dimension=0, tiled=True
        ).astype(jnp.float32),
        lax.psum_scatter(
            columns[4].astype(jnp.bfloat16), "batch", scatter_dimension=0, tiled=True
        ).astype(jnp.float32),
        lax.psum_scatter(
            columns[5].astype(jnp.bfloat16), "batch", scatter_dimension=0, tiled=True
        ).astype(jnp.float32),
        lax.psum_scatter(
            columns[6].astype(jnp.bfloat16), "batch", scatter_dimension=0, tiled=True
        ).astype(jnp.float32),
    )
    squares = jnp.stack(
        [
            jnp.sum(inputs * inputs),
            jnp.sum(attn_branch * attn_branch),
            jnp.sum(mlp_branch * mlp_branch),
        ]
    )
    gain_a_grad, gain_m_grad, totals = lax.psum(
        (gain_a_part, gain_m_part, squares), ("batch", "seq")
    )
    entries = seqs_here * local_len * width * lax.axis_size("batch") * lax.axis_size("seq")
    residual_rms = jnp.sqrt(totals / entries)
    return (
        layer_output,
        input_grad,
        gain_a_grad,
        owned[0],
        owned[1],
        owned[2],
        owned[3],
        gain_m_grad,
        owned[4],
        owned[5],
        owned[6],
        residual_rms,
    )


def solution(mesh):
    in_specs = (
        P("batch", "seq", None),
        P("batch"),
        P(),
        P("batch", "seq"),
        P("batch", "seq"),
        P("batch", "seq"),
        P("batch", "seq"),
        P(),
        P("batch", "seq"),
        P("batch", "seq"),
        P("batch", "seq"),
        P("batch", "seq", None),
    )
    out_specs = (
        P("batch", "seq", None),
        P("batch", "seq", None),
        P(),
        P("batch", "seq"),
        P("batch", "seq"),
        P("batch", "seq"),
        P("batch", "seq"),
        P(),
        P("batch", "seq"),
        P("batch", "seq"),
        P("batch", "seq"),
        P(),
    )
    return jax.shard_map(
        on_device, mesh=mesh, in_specs=in_specs, out_specs=out_specs, check_vma=False
    )
```

profile of v0, /device:TPU:0, one launch (start us, length us, event | category | flops | bytes accessed | tf_op | source)
XLA Modules:
  0.0 1683.6 jit_solution(3768329245522326956)
XLA Ops:
  10.6 16.8 all_gather.92
  27.6 13.3 all_gather.93
  43.3 15.4 all_gather.95
  58.9 13.3 all_gather.96
  74.0 22.7 %all_gather.90 = bf16[1152,288]{1,0:T(8,128)(2,1)S(1)} all-gather(bf16[144,288]{1,0:T(8,128)(2,1)S(1)} %copy-done.17), channel_id=1, replica_groups=mesh['batch'=8,'seq'=4] {'batch'}, dimensions={0}, use_global_device_ids=true | all-gather | bytes 746496 | tf_op jit(solution)/shard_map/all_gather | solution.py:40
  97.9 16.3 all_gather.98
  117.4 11.7 all-gather.47.cloned.1.call-done
  129.2 27.3 %all-gather.43.cloned.1.call-done = bf16[1152,768]{1,0:T(8,128)(2,1)} async-done(((bf16[144,768]{1,0:T(8,128)(2,1)}), bf16[1152,768]{1,0:T(8,128)(2,1)}) %all-gather.43.cloned.1.call-update) | async-done | bytes 1769488 | tf_op jit(solution)/shard_map/all_gather | solution.py:44
  156.6 15.9 all_gather.112
  175.4 13.5 all-gather.21.cloned.1.call-done
  190.5 31.7 %all-gather.23.cloned.1.call-done = bf16[2,1024,384]{2,1,0:T(8,128)(2,1)} async-done(((bf16[2,256,384]{2,1,0:T(8,128)(2,1)}), bf16[2,1024,384]{2,1,0:T(8,128)(2,1)}) %all-gather.23.cloned.1.call-update) | async-done | bytes 1572880 | tf_op jit(solution)/shard_map/all_gather | solution.py:192
  225.2 39.2 %all-gather.19.cloned.1.call-done = bf16[1152,1152]{0,1:T(8,128)(2,1)} async-done(((bf16[1152,288]{0,1:T(8,128)(2,1)}), bf16[1152,1152]{0,1:T(8,128)(2,1)}) %all-gather.19.cloned.1.call-update) | async-done | bytes 2654224 | tf_op jit(solution)/shard_map/all_gather | solution.py:49
  269.0 43.9 %while.30 = (s32[]{:T(128)}, bf16[6,2,3,256,64]{3,4,2,0,1:T(8,128)(2,1)}, f32[6,2,3,256]{3,2,1,0:T(4,128)S(1)}, bf16[6,2,3,256,64]{3,4,2,1,0:T(8,128)(2,1)S(1)},...) while((s32[]{:T(128)}, ...), condition=%wide.region_4.5_spmd.clone.clone, body=%wide.region_1.4_spmd.clone.sunk.clone | while | flops 422050304 | bytes 22407264 | solution.py:201
  321.3 63.1 %all-gather.41.cloned.1.call-done = bf16[3072,1152]{0,1:T(8,128)(2,1)} async-done(((bf16[3072,288]{0,1:T(8,128)(2,1)}), bf16[3072,1152]{0,1:T(8,128)(2,1)}) %all-gather.41.cloned.1.call-update) | async-done | bytes 7077904 | tf_op jit(solution)/shard_map/all_gather | solution.py:55
  384.4 10.7 fusion.66
  395.1 67.7 %all-gather.29.cloned.1.call-done = bf16[1152,3072]{1,0:T(8,128)(2,1)} async-done(((bf16[1152,768]{1,0:T(8,128)(2,1)}), bf16[1152,3072]{1,0:T(8,128)(2,1)}) %all-gather.29.cloned.1.call-update) | async-done | bytes 7077904 | tf_op jit(solution)/shard_map/all_gather | solution.py:53
  462.8 10.7 fusion.72
  473.6 67.6 %all-gather.33.cloned.1.call-done = bf16[1152,3072]{1,0:T(8,128)(2,1)} async-done(((bf16[1152,768]{1,0:T(8,128)(2,1)}), bf16[1152,3072]{1,0:T(8,128)(2,1)}) %all-gather.33.cloned.1.call-update) | async-done | bytes 7077904 | tf_op jit(solution)/shard_map/all_gather | solution.py:54
  541.1 14.2 fusion.76
  555.3 64.3 %all-gather.49.cloned.1.call-done = bf16[1152,3072]{1,0:T(8,128)(2,1)} async-done(((bf16[1152,768]{1,0:T(8,128)(2,1)}), bf16[1152,3072]{1,0:T(8,128)(2,1)}) %all-gather.49.cloned.1.call-update) | async-done | bytes 7077904 | tf_op jit(solution)/shard_map/all_gather | solution.py:54
  619.6 9.6 fusion.62
  629.2 68.7 %all-gather.45.cloned.1.call-done = bf16[1152,3072]{1,0:T(8,128)(2,1)} async-done(((bf16[1152,768]{1,0:T(8,128)(2,1)}), bf16[1152,3072]{1,0:T(8,128)(2,1)}) %all-gather.45.cloned.1.call-update) | async-done | bytes 7077904 | tf_op jit(solution)/shard_map/all_gather | solution.py:53
  697.9 9.0 fusion.87
  710.7 28.7 %all-gather.51.cloned.1.call-done = bf16[1152,1152]{0,1:T(8,128)(2,1)} async-done(((bf16[1152,288]{0,1:T(8,128)(2,1)}), bf16[1152,1152]{0,1:T(8,128)(2,1)}) %all-gather.51.cloned.1.call-update) | async-done | bytes 2654224 | tf_op jit(solution)/shard_map/all_gather | solution.py:52
  747.1 80.7 %while.31 = (s32[]{:T(128)}, f32[6,2,3,256,64]{3,4,2,0,1:T(8,128)}, bf16[6,2,1024,64]{2,3,0,1:T(8,128)(2,1)}, bf16[6,2,1024,64]{2,3,0,1:T(8,128)(2,1)}, bf16[6,2...) while((s32[]{:T(128)}, f32[6,2,3,256,64]{3,4,2,0,1:T(8,128)}, ...), condition=%wide.region_9.10_spmd.clone.clone, body=%wide.region_7.9_spmd.clone.sunk.clone | while | flops 1030978048 | bytes 52610168 | solution.py:237
  829.0 30.1 %reduce-scatter.27.cloned.1.call-done = bf16[2,256,384]{1,2,0:T(8,128)(2,1)} async-done(((bf16[2,1024,384]{1,2,0:T(8,128)(2,1)}), bf16[2,256,384]{1,2,0:T(8,128)(2,1)}) %reduce-scatter.27.cloned.1.call-update) | async-done | bytes 393232 | tf_op jit(solution)/shard_map/reduce_scatter | solution.py:243
  863.0 30.2 %reduce-scatter.29.cloned.1.call-done = bf16[2,256,384]{1,2,0:T(8,128)(2,1)} async-done(((bf16[2,1024,384]{1,2,0:T(8,128)(2,1)}), bf16[2,256,384]{1,2,0:T(8,128)(2,1)}) %reduce-scatter.29.cloned.1.call-update) | async-done | bytes 393232 | tf_op jit(solution)/shard_map/reduce_scatter | solution.py:246
  909.1 7.9 bitcast_convert_fusion
  926.0 7.7 bitcast_convert_fusion.1
  934.5 15.7 all_gather.114
  954.0 26.0 %reduce-scatter.35.cloned.1.call-done = bf16[1152,96]{0,1:T(8,128)(2,1)} async-done(((bf16[1152,384]{0,1:T(8,128)(2,1)}), bf16[1152,96]{0,1:T(8,128)(2,1)}) %reduce-scatter.35.cloned.1.call-update) | async-done | bytes 221200 | tf_op jit(solution)/shard_map/reduce_scatter | solution.py:276
  981.9 41.0 %reduce-scatter.31.cloned.1.call-done = bf16[1152,288]{0,1:T(8,128)(2,1)} async-done(((bf16[1152,1152]{0,1:T(8,128)(2,1)}), bf16[1152,288]{0,1:T(8,128)(2,1)}) %reduce-scatter.31.cloned.1.call-update) | async-done | bytes 663568 | tf_op jit(solution)/shard_map/reduce_scatter | solution.py:270
  1025.3 40.5 %reduce-scatter.37.cloned.1.call-done = bf16[1152,288]{0,1:T(8,128)(2,1)} async-done(((bf16[1152,1152]{0,1:T(8,128)(2,1)}), bf16[1152,288]{0,1:T(8,128)(2,1)}) %reduce-scatter.37.cloned.1.call-update) | async-done | bytes 663568 | tf_op jit(solution)/shard_map/reduce_scatter | solution.py:279
  1068.2 77.3 %reduce-scatter.47.cloned.1.call-done = bf16[3072,288]{0,1:T(8,128)(2,1)} async-done(((bf16[3072,1152]{0,1:T(8,128)(2,1)}), bf16[3072,288]{0,1:T(8,128)(2,1)}) %reduce-scatter.47.cloned.1.call-update) | async-done | bytes 1769488 | tf_op jit(solution)/shard_map/reduce_scatter | solution.py:288
  1149.5 75.4 %reduce-scatter.39.cloned.1.call-done = bf16[1152,768]{1,0:T(8,128)(2,1)} async-done(((bf16[1152,3072]{1,0:T(8,128)(2,1)}), bf16[1152,768]{1,0:T(8,128)(2,1)}) %reduce-scatter.39.cloned.1.call-update) | async-done | bytes 1769488 | tf_op jit(solution)/shard_map/reduce_scatter | solution.py:282
  1225.0 14.4 all_gather.116
  1239.6 65.0 %reduce-scatter.43.cloned.1.call-done = bf16[1152,768]{1,0:T(8,128)(2,1)} async-done(((bf16[1152,3072]{1,0:T(8,128)(2,1)}), bf16[1152,768]{1,0:T(8,128)(2,1)}) %reduce-scatter.43.cloned.1.call-update) | async-done | bytes 1769488 | tf_op jit(solution)/shard_map/reduce_scatter | solution.py:285
  1304.6 14.3 all_gather.118
  1319.1 16.5 all_gather.117
  1335.6 20.1 %all_gather.119 = bf16[1152,384]{0,1:T(8,128)(2,1)} all-gather(bf16[1152,96]{0,1:T(8,128)(2,1)S(1)} %copy.109), channel_id=1, replica_groups=mesh['batch'=8,'seq'=4] {'seq'}, dimensions={1}, use_global_device_ids=true | all-gather | bytes 1105920 | tf_op jit(solution)/shard_map/all_gather | solution.py:51
  1359.7 74.4 %all-gather.37.cloned.1.call-done = bf16[3072,1152]{0,1:T(8,128)(2,1)} async-done(((bf16[3072,288]{0,1:T(8,128)(2,1)}), bf16[3072,1152]{0,1:T(8,128)(2,1)}) %all-gather.37.cloned.1.call-update) | async-done | bytes 7077904 | tf_op jit(solution)/shard_map/all_gather | solution.py:55
  1434.0 11.4 multiply_reduce_fusion.1
  1450.5 39.7 %all-reduce = (f32[1152]{0:T(1024)}, f32[1152]{0:T(1024)}, f32[3]{0:T(128)}) all-reduce(f32[1152]{0:T(1024)S(1)} %get-tuple-element.244, f32[1152]{0:T(1024)} %get-tuple-element.302, f32[3]{0:T(128)S(1)} %pad_maximum_fusion.3), channel_id=1, replica_groups=mesh['batch'=8,'seq'=4] {'batch','seq'}, use_global_device_ids=true, to_apply=%region_14.15 | all-reduce | flops 2307 | bytes 18456 | tf_op jit(solution)/shard_map/psum | solution.py:322
  1501.3 30.8 %reduce-scatter.49.cloned.1.call-done = bf16[144,288]{1,0:T(8,128)(2,1)} async-done(((bf16[1152,288]{1,0:T(8,128)(2,1)}), bf16[144,288]{1,0:T(8,128)(2,1)}) %reduce-scatter.49.cloned.1.call-update) | async-done | bytes 82960
  1534.0 31.0 %reduce-scatter.55.cloned.1.call-done = bf16[144,288]{1,0:T(8,128)(2,1)} async-done(((bf16[1152,288]{1,0:T(8,128)(2,1)}), bf16[144,288]{1,0:T(8,128)(2,1)}) %reduce-scatter.55.cloned.1.call-update) | async-done | bytes 82960
  1566.7 35.9 %reduce-scatter.57.cloned.1.call-done = bf16[384,288]{1,0:T(8,128)(2,1)} async-done(((bf16[3072,288]{1,0:T(8,128)(2,1)}), bf16[384,288]{1,0:T(8,128)(2,1)}) %reduce-scatter.57.cloned.1.call-update) | async-done | bytes 221200
  1604.6 34.4 %reduce-scatter.41.cloned.1.call-done = bf16[144,768]{1,0:T(8,128)(2,1)} async-done(((bf16[1152,768]{1,0:T(8,128)(2,1)}), bf16[144,768]{1,0:T(8,128)(2,1)}) %reduce-scatter.41.cloned.1.call-update) | async-done | bytes 221200 | tf_op jit(solution)/shard_map/reduce_scatter | solution.py:305
  1640.7 33.8 %reduce-scatter.45.cloned.1.call-done = bf16[144,768]{1,0:T(8,128)(2,1)} async-done(((bf16[1152,768]{1,0:T(8,128)(2,1)}), bf16[144,768]{1,0:T(8,128)(2,1)}) %reduce-scatter.45.cloned.1.call-update) | async-done | bytes 221200 | tf_op jit(solution)/shard_map/reduce_scatter | solution.py:308
  (292 shorter events, 242.4 us)
Async XLA Ops:
  7.2 33.8 %copy-start = (bf16[2,256,1152]{2,1,0:T(8,128)(2,1)S(1)}, bf16[2,256,1152]{2,1,0:T(8,128)(2,1)}, u32[]{:S(2)}) copy-start(bf16[2,256,1152]{2,1,0:T(8,128)(2,1)} %param.16) | copy-start | bytes 3538948
  7.2 34.3 %copy-start.29 = (f32[1152]{0:T(1024)S(1)}, f32[1152]{0:T(1024)}, u32[]{:S(2)}) copy-start(f32[1152]{0:T(1024)} %param.18) | copy-start | bytes 13828
  7.2 108.3 %all-gather.39.cloned.1.call-start = ((), (), s32[]{:S(2)}) async-start(), calls=%async_computation.26 | async-start | bytes 1990656 | tf_op jit(solution)/shard_map/all_gather | solution.py:46
  7.9 108.1 %all-gather.27.cloned.1.call-start = ((), (), s32[]{:S(2)}) async-start(), calls=%async_computation.20 | async-start | bytes 1990656 | tf_op jit(solution)/shard_map/all_gather | solution.py:44
  8.7 108.1 %all-gather.31.cloned.1.call-start = ((), (), s32[]{:S(2)}) async-start(), calls=%async_computation.22 | async-start | bytes 1990656 | tf_op jit(solution)/shard_map/all_gather | solution.py:45
  9.4 119.7 %all-gather.47.cloned.1.call-start = ((), (), s32[]{:S(2)}) async-start(), calls=%async_computation.30 | async-start | bytes 1990656 | tf_op jit(solution)/shard_map/all_gather | solution.py:45
  10.0 146.5 %all-gather.43.cloned.1.call-start = ((), (), s32[]{:S(2)}) async-start(), calls=%async_computation.28 | async-start | bytes 1990656 | tf_op jit(solution)/shard_map/all_gather | solution.py:44
  10.6 178.3 %all-gather.21.cloned.1.call-start = ((), (), s32[]{:S(2)}) async-start(), calls=%async_computation.17 | async-start | bytes 1966080 | tf_op jit(solution)/shard_map/all_gather | solution.py:191
  41.3 223.1 %copy-start.23 = (f32[2,256]{1,0:T(2,128)}, f32[2,256]{1,0:T(2,128)S(1)}, u32[]{:S(2)}) copy-start(f32[2,256]{1,0:T(2,128)S(1)} %add_rsqrt_fusion.1) | copy-start | bytes 6148
  41.5 226.8 %copy-start.12 = (f32[256,32]{0,1:T(8,128)}, f32[256,32]{0,1:T(8,128)S(1)}, u32[]{:S(2)}) copy-start(f32[256,32]{0,1:T(8,128)S(1)} %get-tuple-element.307) | copy-start | bytes 98308
  41.5 226.8 %copy-start.14 = (f32[256,32]{0,1:T(8,128)}, f32[256,32]{0,1:T(8,128)S(1)}, u32[]{:S(2)}) copy-start(f32[256,32]{0,1:T(8,128)S(1)} %get-tuple-element.308) | copy-start | bytes 98308
  43.3 178.9 %all-gather.23.cloned.1.call-start = ((), (), s32[]{:S(2)}) async-start(), calls=%async_computation.18 | async-start | bytes 1966080 | tf_op jit(solution)/shard_map/all_gather | solution.py:192
  73.9 24.0 %copy-start.16 = (bf16[144,288]{1,0:T(8,128)(2,1)S(1)}, bf16[144,288]{1,0:T(8,128)(2,1)}, u32[]{:S(2)}) copy-start(bf16[144,288]{1,0:T(8,128)(2,1)} %param.22) | copy-start | bytes 248836
  73.9 190.5 %all-gather.19.cloned.1.call-start = ((), (), s32[]{:S(2)}) async-start(), calls=%async_computation.16 | async-start | bytes 3317760 | tf_op jit(solution)/shard_map/all_gather | solution.py:49
  97.8 215.1 %all-gather.25.cloned.1.call-start = ((), (), s32[]{:S(2)}) async-start(), calls=%async_computation.19 | async-start | bytes 3317760 | tf_op jit(solution)/shard_map/all_gather | solution.py:52
  115.4 269.0 %all-gather.41.cloned.1.call-start = ((), (), s32[]{:S(2)}) async-start(), calls=%async_computation.27 | async-start | bytes 8847360 | tf_op jit(solution)/shard_map/all_gather | solution.py:55
  116.0 346.8 %all-gather.29.cloned.1.call-start = ((), (), s32[]{:S(2)}) async-start(), calls=%async_computation.21 | async-start | bytes 8847360 | tf_op jit(solution)/shard_map/all_gather | solution.py:53
  116.7 424.4 %all-gather.33.cloned.1.call-start = ((), (), s32[]{:S(2)}) async-start(), calls=%async_computation.23 | async-start | bytes 8847360 | tf_op jit(solution)/shard_map/all_gather | solution.py:54
  117.3 502.3 %all-gather.49.cloned.1.call-start = ((), (), s32[]{:S(2)}) async-start(), calls=%async_computation.31 | async-start | bytes 8847360 | tf_op jit(solution)/shard_map/all_gather | solution.py:54
  129.1 568.8 %all-gather.45.cloned.1.call-start = ((), (), s32[]{:S(2)}) async-start(), calls=%async_computation.29 | async-start | bytes 8847360 | tf_op jit(solution)/shard_map/all_gather | solution.py:53
  156.5 582.9 %all-gather.51.cloned.1.call-start = ((), (), s32[]{:S(2)}) async-start(), calls=%async_computation.32 | async-start | bytes 3317760 | tf_op jit(solution)/shard_map/all_gather | solution.py:52
  173.7 685.5 %reduce-scatter.27.cloned.1.call-start = ((), (), s32[]{:S(2)}) async-start(), calls=%async_computation.34 | async-start | bytes 1966080 | tf_op jit(solution)/shard_map/reduce_scatter | solution.py:243
  827.8 32.4 %copy-start.13 = (f32[256,32]{0,1:T(8,128)S(1)}, f32[256,32]{0,1:T(8,128)}, u32[]{:S(2)}) copy-start(f32[256,32]{0,1:T(8,128)} %copy-done.12) | copy-start | bytes 98308
  827.8 32.4 %copy-start.15 = (f32[256,32]{0,1:T(8,128)S(1)}, f32[256,32]{0,1:T(8,128)}, u32[]{:S(2)}) copy-start(f32[256,32]{0,1:T(8,128)} %copy-done.14) | copy-start | bytes 98308
  827.8 65.3 %reduce-scatter.29.cloned.1.call-start = ((), (), s32[]{:S(2)}) async-start(), calls=%async_computation.35 | async-start | bytes 1966080 | tf_op jit(solution)/shard_map/reduce_scatter | solution.py:246
  827.9 33.3 %copy-start.1 = (bf16[2,256,1152]{2,1,0:T(8,128)(2,1)S(1)}, bf16[2,256,1152]{2,1,0:T(8,128)(2,1)}, u32[]{:S(2)}) copy-start(bf16[2,256,1152]{2,1,0:T(8,128)(2,1)} %param.16) | copy-start | bytes 3538948
  827.9 33.2 %copy-start.24 = (f32[2,256]{1,0:T(2,128)S(1)}, f32[2,256]{1,0:T(2,128)}, u32[]{:S(2)}) copy-start(f32[2,256]{1,0:T(2,128)} %copy-done.23) | copy-start | bytes 6148
  827.9 33.2 %copy-start.30 = (f32[1152]{0:T(1024)S(1)}, f32[1152]{0:T(1024)}, u32[]{:S(2)}) copy-start(f32[1152]{0:T(1024)} %param.18) | copy-start | bytes 13828
  828.4 123.1 %all-gather.35.cloned.1.call-start = ((), (), s32[]{:S(2)}) async-start(), calls=%async_computation.24 | async-start | bytes 1990656 | tf_op jit(solution)/shard_map/all_gather | solution.py:46
  829.0 123.1 %reduce-scatter.33.cloned.1.call-start = ((), (), s32[]{:S(2)}) async-start(), calls=%async_computation.37 | async-start | bytes 1105920 | tf_op jit(solution)/shard_map/reduce_scatter | solution.py:273
  862.9 33.1 %copy-start.7 = (f32[6,2,3,256,64]{3,4,2,0,1:T(8,128)S(1)}, f32[6,2,3,256,64]{3,4,2,0,1:T(8,128)}, u32[]{:S(2)}) copy-start(f32[6,2,3,256,64]{3,4,2,0,1:T(8,128)} %get-tuple-element.117) | copy-start | bytes 7077892
  862.9 117.1 %reduce-scatter.35.cloned.1.call-start = ((), (), s32[]{:S(2)}) async-start(), calls=%async_computation.38 | async-start | bytes 1105920 | tf_op jit(solution)/shard_map/reduce_scatter | solution.py:276
  896.0 126.9 %reduce-scatter.31.cloned.1.call-start = ((), (), s32[]{:S(2)}) async-start(), calls=%async_computation.36 | async-start | bytes 3317760 | tf_op jit(solution)/shard_map/reduce_scatter | solution.py:270
  901.7 164.1 %reduce-scatter.37.cloned.1.call-start = ((), (), s32[]{:S(2)}) async-start(), calls=%async_computation.39 | async-start | bytes 3317760 | tf_op jit(solution)/shard_map/reduce_scatter | solution.py:279
  907.9 237.6 %reduce-scatter.47.cloned.1.call-start = ((), (), s32[]{:S(2)}) async-start(), calls=%async_computation.44 | async-start | bytes 8847360 | tf_op jit(solution)/shard_map/reduce_scatter | solution.py:288
  917.0 307.9 %reduce-scatter.39.cloned.1.call-start = ((), (), s32[]{:S(2)}) async-start(), calls=%async_computation.40 | async-start | bytes 8847360 | tf_op jit(solution)/shard_map/reduce_scatter | solution.py:282
  925.9 378.7 %reduce-scatter.43.cloned.1.call-start = ((), (), s32[]{:S(2)}) async-start(), calls=%async_computation.42 | async-start | bytes 8847360 | tf_op jit(solution)/shard_map/reduce_scatter | solution.py:285
  933.6 422.0 %all-gather.53.cloned.1.call-start = ((), (), s32[]{:S(2)}) async-start(), calls=%async_computation.33 | async-start | bytes 3317760 | tf_op jit(solution)/shard_map/all_gather | solution.py:49
  951.4 482.6 %all-gather.37.cloned.1.call-start = ((), (), s32[]{:S(2)}) async-start(), calls=%async_computation.25 | async-start | bytes 8847360 | tf_op jit(solution)/shard_map/all_gather | solution.py:55
  952.0 543.5 %reduce-scatter.51.cloned.1.call-start = ((), (), s32[]{:S(2)}) async-start(), calls=%async_computation.46 | async-start | bytes 331776
  953.9 545.8 %reduce-scatter.53.cloned.1.call-start = ((), (), s32[]{:S(2)}) async-start(), calls=%async_computation.47 | async-start | bytes 331776
  981.9 550.3 %reduce-scatter.49.cloned.1.call-start = ((), (), s32[]{:S(2)}) async-start(), calls=%async_computation.45 | async-start | bytes 995328
  1025.3 539.7 %reduce-scatter.55.cloned.1.call-start = ((), (), s32[]{:S(2)}) async-start(), calls=%async_computation.48 | async-start | bytes 995328
  1068.1 534.5 %reduce-scatter.57.cloned.1.call-start = ((), (), s32[]{:S(2)}) async-start(), calls=%async_computation.49 | async-start | bytes 2654208
  1149.4 75.6 %copy-start.20 = (bf16[144,96]{1,0:T(8,128)(2,1)S(1)}, bf16[144,96]{1,0:T(8,128)(2,1)}, u32[]{:S(2)}) copy-start(bf16[144,96]{1,0:T(8,128)(2,1)} %param.20) | copy-start | bytes 82948
  1149.5 155.1 %copy-start.22 = (bf16[144,96]{1,0:T(8,128)(2,1)S(1)}, bf16[144,96]{1,0:T(8,128)(2,1)}, u32[]{:S(2)}) copy-start(bf16[144,96]{1,0:T(8,128)(2,1)} %param.21) | copy-start | bytes 82948
  1149.5 489.5 %reduce-scatter.41.cloned.1.call-start = ((), (), s32[]{:S(2)}) async-start(), calls=%async_computation.41 | async-start | bytes 1990656 | tf_op jit(solution)/shard_map/reduce_scatter | solution.py:305
  1224.9 449.6 %reduce-scatter.45.cloned.1.call-start = ((), (), s32[]{:S(2)}) async-start(), calls=%async_computation.43 | async-start | bytes 1990656 | tf_op jit(solution)/shard_map/reduce_scatter | solution.py:308
  (19 other events, 86.7 us)
Sparse Core Ops, SparseCore 0:
  9.6 30.1 all-gather.38
  41.5 26.9 all-gather.26
  70.1 31.7 all-gather.30
  103.4 25.6 all-gather.46
  130.6 25.8 all-gather.42
  158.7 30.1 all-gather.20
  191.3 30.8 all-gather.22
  224.6 39.7 all-gather.18
  266.3 39.7 all-gather.24
  307.8 76.5 all-gather.40
  386.2 76.5 all-gather.28
  464.5 76.5 all-gather.32
  543.0 76.5 all-gather.48
  621.3 76.5 all-gather.44
  699.6 39.7 all-gather.50
  828.0 31.1 reduce-scatter.26
  862.0 31.1 reduce-scatter.28
  894.6 26.4 all-gather.34
  924.1 26.2 reduce-scatter.32
  953.1 26.8 reduce-scatter.34
  983.0 39.8 reduce-scatter.30
  1025.9 39.8 reduce-scatter.36
  1068.8 76.5 reduce-scatter.46
  1148.3 76.5 reduce-scatter.38
  1228.0 76.5 reduce-scatter.42
  1306.8 48.7 all-gather.52
  1357.3 76.6 all-gather.36
  1436.8 30.9 reduce-scatter.50
  1470.6 29.0 reduce-scatter.52
  1501.8 30.2 reduce-scatter.48
  1534.5 30.4 reduce-scatter.54
  1567.2 35.3 reduce-scatter.56
  1604.8 34.1 reduce-scatter.40
  1641.3 33.2 reduce-scatter.44
where the time goes:
time: 1690 us; the launch traced here: 1680 us
  waiting for transfers between devices  1120 us (66%)
  blocking collectives  235 us (14%)
  matrix products  224 us (13%)
  other arithmetic  46.1 us (3%)
  local copies, waits for them, and re-layouts  42.3 us (3%)
    all_gather x2, waiting for transfers between devices, gather_weights(): lax.all_gather(rows[6], 'seq', axis=1, tiled=True)  137 us
    all_gather x2, waiting for transfers between devices, gather_weights(): lax.all_gather(rows[4], 'seq', axis=1, tiled=True)  136 us
    all_gather x2, waiting for transfers between devices, gather_weights(): lax.all_gather(rows[5], 'seq', axis=1, tiled=True)  132 us
    unnamed x39, waiting for transfers between devices  107 us
    reduce_scatter x1, waiting for transfers between devices, on_device(): lax.psum_scatter(grad_down.astype(jnp.bfloat16), 'seq', scatter_dimension...  77.3 us
    reduce_scatter x1, waiting for transfers between devices, on_device(): lax.psum_scatter(grad_gate.astype(jnp.bfloat16), 'seq', scatter_dimension...  75.4 us
    reduce_scatter x1, waiting for transfers between devices, on_device(): lax.psum_scatter(upper_half_gradient.astype(jnp.bfloat16), 'seq', scatter...  65 us
    dot_general x7, matrix products, apply_projection(): jnp.einsum('jnh,hb->jnb', left_operand, right_operand, preferred_element_...  48.3 us
  transfers between devices with their start and end apart: 34, of which 26 were waited for; matrix products, arithmetic and copies ran while one was open for 13% of the time, Pallas kernels for 0%

commit v1 on v0

--- a/solution.py
+++ b/solution.py
@@ -9,6 +9,11 @@
 SEQ_LEN = 1024
 EPSILON = 1e-05
 MASKED = -1e30
+
+
+def gather_by_exchange(value, axis, dim):
+    copies = jnp.concatenate([value] * lax.axis_size(axis), axis=dim)
+    return lax.all_to_all(copies, axis, dim, dim, tiled=True)
 
 
 def rope_tables(positions, half_width):
@@ -52,7 +57,7 @@
         lax.all_gather(rows[3], "seq", axis=1, tiled=True),
         lax.all_gather(rows[4], "seq", axis=1, tiled=True),
         lax.all_gather(rows[5], "seq", axis=1, tiled=True),
-        lax.all_gather(rows[6], "seq", axis=1, tiled=True),
+        gather_by_exchange(rows[6], "seq", 1),
     )
 
 

time: 1690 us -> 1680 us (level)
  waiting for transfers between devices: 1120 us -> 1080 us
    all_gather x2 -> x0, waiting for transfers between devices: 137 us -> none  [gather_weights(): lax.all_gather(rows[6], 'seq', axis=1, tiled=True)]
    reduce_scatter x1, waiting for transfers between devices: 75.4 us -> 139 us  [on_device(): lax.psum_scatter(grad_gate.astype(jnp.bfloat16), 'seq', scatter_dimension...]
    all_gather x2, waiting for transfers between devices: 0.03 us -> 49.1 us  [gather_weights(): lax.all_gather(weights[6], 'batch', axis=0, tiled=True)]
    all_gather x2, waiting for transfers between devices: 39.2 us -> 86.3 us  [gather_weights(): lax.all_gather(rows[0], 'seq', axis=1, tiled=True)]
    reduce_scatter x1, waiting for transfers between devices: 26 us -> 0.02 us  [on_device(): lax.psum_scatter(value_gradient_rows.astype(jnp.bfloat16), 'seq', scatter...]
    unnamed x39 -> x37, waiting for transfers between devices: 107 us -> 103 us
  transfers between devices with their start and end apart: 34 -> 34, of which waited for: 26 -> 24; matrix products, arithmetic and copies ran while one was open for 13% -> 14% of each run, Pallas kernels for 0% -> 0%
where the time goes in v1:
time: 1680 us; the launch traced here: 1670 us
  waiting for transfers between devices  1080 us (64%)
  blocking collectives  234 us (14%)
  matrix products  224 us (13%)
  other arithmetic  59.6 us (4%)
  local copies, waits for them, and re-layouts  41.7 us (2%)
    reduce_scatter x1, waiting for transfers between devices, on_device(): lax.psum_scatter(grad_gate.astype(jnp.bfloat16), 'seq', scatter_dimension...  139 us
    all_gather x2, waiting for transfers between devices, gather_weights(): lax.all_gather(rows[5], 'seq', axis=1, tiled=True)  132 us
    all_gather x2, waiting for transfers between devices, gather_weights(): lax.all_gather(rows[4], 'seq', axis=1, tiled=True)  128 us
    unnamed x37, waiting for transfers between devices  103 us
    all_gather x2, waiting for transfers between devices, gather_weights(): lax.all_gather(rows[0], 'seq', axis=1, tiled=True)  86.3 us
    reduce_scatter x1, waiting for transfers between devices, on_device(): lax.psum_scatter(grad_down.astype(jnp.bfloat16), 'seq', scatter_dimension...  77.2 us
    reduce_scatter x1, waiting for transfers between devices, on_device(): lax.psum_scatter(upper_half_gradient.astype(jnp.bfloat16), 'seq', scatter...  64.9 us
    all_gather x2, waiting for transfers between devices, gather_weights(): lax.all_gather(weights[6], 'batch', axis=0, tiled=True)  49.1 us
  transfers between devices with their start and end apart: 34, of which 24 were waited for; matrix products, arithmetic and copies ran while one was open for 14% of the time, Pallas kernels for 0%

profile of v1, /device:TPU:0, one launch (start us, length us, event | category | flops | bytes accessed | tf_op | source)
XLA Modules:
  0.0 1667.5 jit_solution(2205391646665155050)
XLA Ops:
  10.0 16.5 all_gather.86
  26.7 13.3 all_gather.87
  42.4 15.6 all_gather.89
  58.1 13.2 all_gather.90
  73.8 22.7 %all_gather.84 = bf16[1152,288]{1,0:T(8,128)(2,1)S(1)} all-gather(bf16[144,288]{1,0:T(8,128)(2,1)S(1)} %copy-done.18), channel_id=1, replica_groups=mesh['batch'=8,'seq'=4] {'batch'}, dimensions={0}, use_global_device_ids=true | all-gather | bytes 746496 | tf_op jit(solution)/shard_map/all_gather | solution.py:45
  97.8 16.3 all_gather.92
  117.3 11.9 all-gather.37.cloned.1.call-done
  129.2 15.9 all_gather.104
  147.8 13.8 all-gather.19.cloned.1.call-done
  163.2 31.5 %all-gather.21.cloned.1.call-done = bf16[2,1024,384]{2,1,0:T(8,128)(2,1)} async-done(((bf16[2,256,384]{2,1,0:T(8,128)(2,1)}), bf16[2,1024,384]{2,1,0:T(8,128)(2,1)}) %all-gather.21.cloned.1.call-update) | async-done | bytes 1572880 | tf_op jit(solution)/shard_map/all_gather | solution.py:197
  197.8 25.0 %all-gather.35.cloned.1.call-done = bf16[3072,288]{0,1:T(8,128)(2,1)} async-done(((bf16[384,288]{0,1:T(8,128)(2,1)}), bf16[3072,288]{0,1:T(8,128)(2,1)}) %all-gather.35.cloned.1.call-update) | async-done | bytes 1769488 | tf_op jit(solution)/shard_map/all_gather | solution.py:51
  222.8 6.8 pad_maximum_fusion.1
  235.5 86.3 %all-gather.17.cloned.1.call-done = bf16[1152,1152]{0,1:T(8,128)(2,1)} async-done(((bf16[1152,288]{0,1:T(8,128)(2,1)}), bf16[1152,1152]{0,1:T(8,128)(2,1)}) %all-gather.17.cloned.1.call-update) | async-done | bytes 2654224 | tf_op jit(solution)/shard_map/all_gather | solution.py:54
  326.1 43.6 %while.30 = (s32[]{:T(128)}, bf16[6,2,3,256,64]{3,4,2,0,1:T(8,128)(2,1)}, f32[6,2,3,256]{3,2,1,0:T(4,128)S(1)}, bf16[6,2,3,256,64]{3,4,2,1,0:T(8,128)(2,1)S(1)},...) while((s32[]{:T(128)}, ...), condition=%wide.region_4.5_spmd.clone.clone, body=%wide.region_1.4_spmd.clone.sunk.clone | while | flops 422050304 | bytes 22407264 | solution.py:206
  382.2 11.2 fusion.121
  393.4 59.3 %all-gather.27.cloned.1.call-done = bf16[1152,3072]{1,0:T(8,128)(2,1)} async-done(((bf16[1152,768]{1,0:T(8,128)(2,1)}), bf16[1152,3072]{1,0:T(8,128)(2,1)}) %all-gather.27.cloned.1.call-update) | async-done | bytes 7077904 | tf_op jit(solution)/shard_map/all_gather | solution.py:58
  452.7 10.8 fusion.68
  463.5 67.7 %all-gather.31.cloned.1.call-done = bf16[1152,3072]{1,0:T(8,128)(2,1)} async-done(((bf16[1152,768]{1,0:T(8,128)(2,1)}), bf16[1152,3072]{1,0:T(8,128)(2,1)}) %all-gather.31.cloned.1.call-update) | async-done | bytes 7077904 | tf_op jit(solution)/shard_map/all_gather | solution.py:59
  531.2 14.2 fusion.72
  545.4 64.1 %all-gather.43.cloned.1.call-done = bf16[1152,3072]{1,0:T(8,128)(2,1)} async-done(((bf16[1152,768]{1,0:T(8,128)(2,1)}), bf16[1152,3072]{1,0:T(8,128)(2,1)}) %all-gather.43.cloned.1.call-update) | async-done | bytes 7077904 | tf_op jit(solution)/shard_map/all_gather | solution.py:59
  609.5 9.6 fusion.62
  619.2 68.8 %all-gather.39.cloned.1.call-done = bf16[1152,3072]{1,0:T(8,128)(2,1)} async-done(((bf16[1152,768]{1,0:T(8,128)(2,1)}), bf16[1152,3072]{1,0:T(8,128)(2,1)}) %all-gather.39.cloned.1.call-update) | async-done | bytes 7077904 | tf_op jit(solution)/shard_map/all_gather | solution.py:58
  688.0 9.0 fusion.83
  700.8 28.7 %all-gather.45.cloned.1.call-done = bf16[1152,1152]{0,1:T(8,128)(2,1)} async-done(((bf16[1152,288]{0,1:T(8,128)(2,1)}), bf16[1152,1152]{0,1:T(8,128)(2,1)}) %all-gather.45.cloned.1.call-update) | async-done | bytes 2654224 | tf_op jit(solution)/shard_map/all_gather | solution.py:57
  737.2 80.7 %while.31 = (s32[]{:T(128)}, f32[6,2,3,256,64]{3,4,2,0,1:T(8,128)}, bf16[6,2,1024,64]{2,3,0,1:T(8,128)(2,1)}, bf16[6,2,1024,64]{2,3,0,1:T(8,128)(2,1)}, bf16[6,2...) while((s32[]{:T(128)}, f32[6,2,3,256,64]{3,4,2,0,1:T(8,128)}, ...), condition=%wide.region_9.10_spmd.clone.clone, body=%wide.region_7.9_spmd.clone.sunk.clone | while | flops 1030978048 | bytes 52610168 | solution.py:242
  818.5 30.7 %reduce-scatter.27.cloned.1.call-done = bf16[2,256,384]{1,2,0:T(8,128)(2,1)} async-done(((bf16[2,1024,384]{1,2,0:T(8,128)(2,1)}), bf16[2,256,384]{1,2,0:T(8,128)(2,1)}) %reduce-scatter.27.cloned.1.call-update) | async-done | bytes 393232 | tf_op jit(solution)/shard_map/reduce_scatter | solution.py:248
  853.0 30.2 %reduce-scatter.29.cloned.1.call-done = bf16[2,256,384]{1,2,0:T(8,128)(2,1)} async-done(((bf16[2,1024,384]{1,2,0:T(8,128)(2,1)}), bf16[2,256,384]{1,2,0:T(8,128)(2,1)}) %reduce-scatter.29.cloned.1.call-update) | async-done | bytes 393232 | tf_op jit(solution)/shard_map/reduce_scatter | solution.py:251
  899.2 7.9 bitcast_convert_fusion
  908.4 7.6 bitcast_convert_fusion.2
  916.1 7.6 bitcast_convert_fusion.1
  924.6 15.7 all_gather.106
  945.4 40.0 %reduce-scatter.31.cloned.1.call-done = bf16[1152,288]{0,1:T(8,128)(2,1)} async-done(((bf16[1152,1152]{0,1:T(8,128)(2,1)}), bf16[1152,288]{0,1:T(8,128)(2,1)}) %reduce-scatter.31.cloned.1.call-update) | async-done | bytes 663568 | tf_op jit(solution)/shard_map/reduce_scatter | solution.py:275
  987.8 40.3 %reduce-scatter.37.cloned.1.call-done = bf16[1152,288]{0,1:T(8,128)(2,1)} async-done(((bf16[1152,1152]{0,1:T(8,128)(2,1)}), bf16[1152,288]{0,1:T(8,128)(2,1)}) %reduce-scatter.37.cloned.1.call-update) | async-done | bytes 663568 | tf_op jit(solution)/shard_map/reduce_scatter | solution.py:284
  1030.5 77.2 %reduce-scatter.47.cloned.1.call-done = bf16[3072,288]{0,1:T(8,128)(2,1)} async-done(((bf16[3072,1152]{0,1:T(8,128)(2,1)}), bf16[3072,288]{0,1:T(8,128)(2,1)}) %reduce-scatter.47.cloned.1.call-update) | async-done | bytes 1769488 | tf_op jit(solution)/shard_map/reduce_scatter | solution.py:293
  1111.8 24.1 %all-gather.33.cloned.1.call-done = bf16[3072,288]{0,1:T(8,128)(2,1)} async-done(((bf16[384,288]{0,1:T(8,128)(2,1)}), bf16[3072,288]{0,1:T(8,128)(2,1)}) %all-gather.33.cloned.1.call-update) | async-done | bytes 1769488 | tf_op jit(solution)/shard_map/all_gather | solution.py:51
  1148.6 138.9 %reduce-scatter.39.cloned.1.call-done = bf16[1152,768]{1,0:T(8,128)(2,1)} async-done(((bf16[1152,3072]{1,0:T(8,128)(2,1)}), bf16[1152,768]{1,0:T(8,128)(2,1)}) %reduce-scatter.39.cloned.1.call-update) | async-done | bytes 1769488 | tf_op jit(solution)/shard_map/reduce_scatter | solution.py:287
  1287.6 14.3 all_gather.108
  1302.1 64.9 %reduce-scatter.43.cloned.1.call-done = bf16[1152,768]{1,0:T(8,128)(2,1)} async-done(((bf16[1152,3072]{1,0:T(8,128)(2,1)}), bf16[1152,768]{1,0:T(8,128)(2,1)}) %reduce-scatter.43.cloned.1.call-update) | async-done | bytes 1769488 | tf_op jit(solution)/shard_map/reduce_scatter | solution.py:290
  1367.1 14.3 all_gather.110
  1381.6 16.6 all_gather.109
  1398.1 20.1 %all_gather.111 = bf16[1152,384]{0,1:T(8,128)(2,1)} all-gather(bf16[1152,96]{0,1:T(8,128)(2,1)S(1)} %copy.115), channel_id=1, replica_groups=mesh['batch'=8,'seq'=4] {'seq'}, dimensions={1}, use_global_device_ids=true | all-gather | bytes 1105920 | tf_op jit(solution)/shard_map/all_gather | solution.py:56
  1422.3 11.4 multiply_reduce_fusion.1
  1438.8 39.6 %all-reduce = (f32[1152]{0:T(1024)}, f32[1152]{0:T(1024)}, f32[3]{0:T(128)}) all-reduce(f32[1152]{0:T(1024)S(1)} %get-tuple-element.244, f32[1152]{0:T(1024)} %get-tuple-element.302, f32[3]{0:T(128)S(1)} %pad_maximum_fusion.5), channel_id=1, replica_groups=mesh['batch'=8,'seq'=4] {'batch','seq'}, use_global_device_ids=true, to_apply=%region_14.15 | all-reduce | flops 2307 | bytes 18456 | tf_op jit(solution)/shard_map/psum | solution.py:327
  1486.9 29.5 %reduce-scatter.49.cloned.1.call-done = bf16[144,288]{1,0:T(8,128)(2,1)} async-done(((bf16[1152,288]{1,0:T(8,128)(2,1)}), bf16[144,288]{1,0:T(8,128)(2,1)}) %reduce-scatter.49.cloned.1.call-update) | async-done | bytes 82960
  1518.2 30.9 %reduce-scatter.55.cloned.1.call-done = bf16[144,288]{1,0:T(8,128)(2,1)} async-done(((bf16[1152,288]{1,0:T(8,128)(2,1)}), bf16[144,288]{1,0:T(8,128)(2,1)}) %reduce-scatter.55.cloned.1.call-update) | async-done | bytes 82960
  1550.9 35.7 %reduce-scatter.57.cloned.1.call-done = bf16[384,288]{1,0:T(8,128)(2,1)} async-done(((bf16[3072,288]{1,0:T(8,128)(2,1)}), bf16[384,288]{1,0:T(8,128)(2,1)}) %reduce-scatter.57.cloned.1.call-update) | async-done | bytes 221200
  1588.6 34.7 %reduce-scatter.41.cloned.1.call-done = bf16[144,768]{1,0:T(8,128)(2,1)} async-done(((bf16[1152,768]{1,0:T(8,128)(2,1)}), bf16[144,768]{1,0:T(8,128)(2,1)}) %reduce-scatter.41.cloned.1.call-update) | async-done | bytes 221200 | tf_op jit(solution)/shard_map/reduce_scatter | solution.py:310
  1625.0 33.8 %reduce-scatter.45.cloned.1.call-done = bf16[144,768]{1,0:T(8,128)(2,1)} async-done(((bf16[1152,768]{1,0:T(8,128)(2,1)}), bf16[144,768]{1,0:T(8,128)(2,1)}) %reduce-scatter.45.cloned.1.call-update) | async-done | bytes 221200 | tf_op jit(solution)/shard_map/reduce_scatter | solution.py:313
  (294 shorter events, 253.3 us)
Async XLA Ops:
  7.2 32.9 %copy-start = (bf16[2,256,1152]{2,1,0:T(8,128)(2,1)S(1)}, bf16[2,256,1152]{2,1,0:T(8,128)(2,1)}, u32[]{:S(2)}) copy-start(bf16[2,256,1152]{2,1,0:T(8,128)(2,1)} %param.16) | copy-start | bytes 3538948
  7.2 33.4 %copy-start.30 = (f32[1152]{0:T(1024)S(1)}, f32[1152]{0:T(1024)}, u32[]{:S(2)}) copy-start(f32[1152]{0:T(1024)} %param.18) | copy-start | bytes 13828
  7.2 108.2 %all-gather.25.cloned.1.call-start = ((), (), s32[]{:S(2)}) async-start(), calls=%async_computation.22 | async-start | bytes 1990656 | tf_op jit(solution)/shard_map/all_gather | solution.py:49
  7.9 108.1 %all-gather.29.cloned.1.call-start = ((), (), s32[]{:S(2)}) async-start(), calls=%async_computation.24 | async-start | bytes 1990656 | tf_op jit(solution)/shard_map/all_gather | solution.py:50
  8.7 108.1 %all-gather.41.cloned.1.call-start = ((), (), s32[]{:S(2)}) async-start(), calls=%async_computation.30 | async-start | bytes 1990656 | tf_op jit(solution)/shard_map/all_gather | solution.py:50
  9.4 119.7 %all-gather.37.cloned.1.call-start = ((), (), s32[]{:S(2)}) async-start(), calls=%async_computation.28 | async-start | bytes 1990656 | tf_op jit(solution)/shard_map/all_gather | solution.py:49
  10.0 151.6 %all-gather.19.cloned.1.call-start = ((), (), s32[]{:S(2)}) async-start(), calls=%async_computation.19 | async-start | bytes 1966080 | tf_op jit(solution)/shard_map/all_gather | solution.py:196
  40.4 281.5 %copy-start.24 = (f32[2,256]{1,0:T(2,128)}, f32[2,256]{1,0:T(2,128)S(1)}, u32[]{:S(2)}) copy-start(f32[2,256]{1,0:T(2,128)S(1)} %add_rsqrt_fusion.1) | copy-start | bytes 6148
  40.6 284.8 %copy-start.13 = (f32[256,32]{0,1:T(8,128)}, f32[256,32]{0,1:T(8,128)S(1)}, u32[]{:S(2)}) copy-start(f32[256,32]{0,1:T(8,128)S(1)} %get-tuple-element.307) | copy-start | bytes 98308
  40.6 284.8 %copy-start.15 = (f32[256,32]{0,1:T(8,128)}, f32[256,32]{0,1:T(8,128)S(1)}, u32[]{:S(2)}) copy-start(f32[256,32]{0,1:T(8,128)S(1)} %get-tuple-element.308) | copy-start | bytes 98308
  42.3 152.4 %all-gather.21.cloned.1.call-start = ((), (), s32[]{:S(2)}) async-start(), calls=%async_computation.20 | async-start | bytes 1966080 | tf_op jit(solution)/shard_map/all_gather | solution.py:197
  73.0 149.8 %all-gather.35.cloned.1.call-start = ((), (), s32[]{:S(2)}) async-start(), calls=%async_computation.27 | async-start | bytes 1990656 | tf_op jit(solution)/shard_map/all_gather | solution.py:51
  73.8 248.1 %all-gather.17.cloned.1.call-start = ((), (), s32[]{:S(2)}) async-start(), calls=%async_computation.18 | async-start | bytes 3317760 | tf_op jit(solution)/shard_map/all_gather | solution.py:54
  97.7 276.7 %all-gather.23.cloned.1.call-start = ((), (), s32[]{:S(2)}) async-start(), calls=%async_computation.21 | async-start | bytes 3317760 | tf_op jit(solution)/shard_map/all_gather | solution.py:57
  115.3 337.4 %all-gather.27.cloned.1.call-start = ((), (), s32[]{:S(2)}) async-start(), calls=%async_computation.23 | async-start | bytes 8847360 | tf_op jit(solution)/shard_map/all_gather | solution.py:58
  115.9 415.3 %all-gather.31.cloned.1.call-start = ((), (), s32[]{:S(2)}) async-start(), calls=%async_computation.25 | async-start | bytes 8847360 | tf_op jit(solution)/shard_map/all_gather | solution.py:59
  116.7 492.8 %all-gather.43.cloned.1.call-start = ((), (), s32[]{:S(2)}) async-start(), calls=%async_computation.31 | async-start | bytes 8847360 | tf_op jit(solution)/shard_map/all_gather | solution.py:59
  117.2 570.7 %all-gather.39.cloned.1.call-start = ((), (), s32[]{:S(2)}) async-start(), calls=%async_computation.29 | async-start | bytes 8847360 | tf_op jit(solution)/shard_map/all_gather | solution.py:58
  129.2 600.3 %all-gather.45.cloned.1.call-start = ((), (), s32[]{:S(2)}) async-start(), calls=%async_computation.32 | async-start | bytes 3317760 | tf_op jit(solution)/shard_map/all_gather | solution.py:57
  229.6 92.2 %copy-start.1 = (bf16[2,256,1152]{2,1,0:T(8,128)(2,1)S(1)}, bf16[2,256,1152]{2,1,0:T(8,128)(2,1)}, u32[]{:S(2)}) copy-start(bf16[2,256,1152]{2,1,0:T(8,128)(2,1)} %param.16) | copy-start | bytes 3538948
  229.6 152.6 %all-to-all-start.1 = ((bf16[3072,4,288]{0,2,1:T(8,128)(2,1)}), bf16[3072,4,288]{0,2,1:T(8,128)(2,1)}, u32[]{:S(2)}, u32[]{:S(2)}) async-start(bf16[3072,4,288]{0,2,1:T(8,128)(2,1)} %bitcast.294), calls=%async_computation.1 | async-start | bytes 14155776 | tf_op jit(solution)/shard_map/all_to_all | solution.py:16
  235.3 613.9 %reduce-scatter.27.cloned.1.call-start = ((), (), s32[]{:S(2)}) async-start(), calls=%async_computation.34 | async-start | bytes 1966080 | tf_op jit(solution)/shard_map/reduce_scatter | solution.py:248
  817.9 32.4 %copy-start.14 = (f32[256,32]{0,1:T(8,128)S(1)}, f32[256,32]{0,1:T(8,128)}, u32[]{:S(2)}) copy-start(f32[256,32]{0,1:T(8,128)} %copy-done.13) | copy-start | bytes 98308
  817.9 32.4 %copy-start.16 = (f32[256,32]{0,1:T(8,128)S(1)}, f32[256,32]{0,1:T(8,128)}, u32[]{:S(2)}) copy-start(f32[256,32]{0,1:T(8,128)} %copy-done.15) | copy-start | bytes 98308
  817.9 65.3 %reduce-scatter.29.cloned.1.call-start = ((), (), s32[]{:S(2)}) async-start(), calls=%async_computation.35 | async-start | bytes 1966080 | tf_op jit(solution)/shard_map/reduce_scatter | solution.py:251
  817.9 33.3 %copy-start.2 = (bf16[2,256,1152]{2,1,0:T(8,128)(2,1)S(1)}, bf16[2,256,1152]{2,1,0:T(8,128)(2,1)}, u32[]{:S(2)}) copy-start(bf16[2,256,1152]{2,1,0:T(8,128)(2,1)} %param.16) | copy-start | bytes 3538948
  818.0 33.3 %copy-start.25 = (f32[2,256]{1,0:T(2,128)S(1)}, f32[2,256]{1,0:T(2,128)}, u32[]{:S(2)}) copy-start(f32[2,256]{1,0:T(2,128)} %copy-done.24) | copy-start | bytes 6148
  818.0 33.2 %copy-start.31 = (f32[1152]{0:T(1024)S(1)}, f32[1152]{0:T(1024)}, u32[]{:S(2)}) copy-start(f32[1152]{0:T(1024)} %param.18) | copy-start | bytes 13828
  818.5 123.1 %reduce-scatter.33.cloned.1.call-start = ((), (), s32[]{:S(2)}) async-start(), calls=%async_computation.37 | async-start | bytes 1105920 | tf_op jit(solution)/shard_map/reduce_scatter | solution.py:278
  852.9 33.1 %copy-start.8 = (f32[6,2,3,256,64]{3,4,2,0,1:T(8,128)S(1)}, f32[6,2,3,256,64]{3,4,2,0,1:T(8,128)}, u32[]{:S(2)}) copy-start(f32[6,2,3,256,64]{3,4,2,0,1:T(8,128)} %get-tuple-element.117) | copy-start | bytes 7077892
  853.0 90.5 %reduce-scatter.35.cloned.1.call-start = ((), (), s32[]{:S(2)}) async-start(), calls=%async_computation.38 | async-start | bytes 1105920 | tf_op jit(solution)/shard_map/reduce_scatter | solution.py:281
  886.0 99.4 %reduce-scatter.31.cloned.1.call-start = ((), (), s32[]{:S(2)}) async-start(), calls=%async_computation.36 | async-start | bytes 3317760 | tf_op jit(solution)/shard_map/reduce_scatter | solution.py:275
  891.7 136.4 %reduce-scatter.37.cloned.1.call-start = ((), (), s32[]{:S(2)}) async-start(), calls=%async_computation.39 | async-start | bytes 3317760 | tf_op jit(solution)/shard_map/reduce_scatter | solution.py:284
  898.0 209.8 %reduce-scatter.47.cloned.1.call-start = ((), (), s32[]{:S(2)}) async-start(), calls=%async_computation.44 | async-start | bytes 8847360 | tf_op jit(solution)/shard_map/reduce_scatter | solution.py:293
  907.2 228.7 %all-gather.33.cloned.1.call-start = ((), (), s32[]{:S(2)}) async-start(), calls=%async_computation.26 | async-start | bytes 1990656 | tf_op jit(solution)/shard_map/all_gather | solution.py:51
  907.9 379.6 %reduce-scatter.39.cloned.1.call-start = ((), (), s32[]{:S(2)}) async-start(), calls=%async_computation.40 | async-start | bytes 8847360 | tf_op jit(solution)/shard_map/reduce_scatter | solution.py:287
  916.0 451.0 %reduce-scatter.43.cloned.1.call-start = ((), (), s32[]{:S(2)}) async-start(), calls=%async_computation.42 | async-start | bytes 8847360 | tf_op jit(solution)/shard_map/reduce_scatter | solution.py:290
  923.7 494.6 %all-gather.47.cloned.1.call-start = ((), (), s32[]{:S(2)}) async-start(), calls=%async_computation.33 | async-start | bytes 3317760 | tf_op jit(solution)/shard_map/all_gather | solution.py:54
  941.5 542.2 %reduce-scatter.51.cloned.1.call-start = ((), (), s32[]{:S(2)}) async-start(), calls=%async_computation.46 | async-start | bytes 331776
  943.4 541.9 %reduce-scatter.53.cloned.1.call-start = ((), (), s32[]{:S(2)}) async-start(), calls=%async_computation.47 | async-start | bytes 331776
  945.4 571.1 %reduce-scatter.49.cloned.1.call-start = ((), (), s32[]{:S(2)}) async-start(), calls=%async_computation.45 | async-start | bytes 995328
  987.8 561.4 %reduce-scatter.55.cloned.1.call-start = ((), (), s32[]{:S(2)}) async-start(), calls=%async_computation.48 | async-start | bytes 995328
  1030.5 556.1 %reduce-scatter.57.cloned.1.call-start = ((), (), s32[]{:S(2)}) async-start(), calls=%async_computation.49 | async-start | bytes 2654208
  1142.5 145.1 %copy-start.21 = (bf16[144,96]{1,0:T(8,128)(2,1)S(1)}, bf16[144,96]{1,0:T(8,128)(2,1)}, u32[]{:S(2)}) copy-start(bf16[144,96]{1,0:T(8,128)(2,1)} %param.20) | copy-start | bytes 82948
  1142.5 279.7 %all-to-all-start = ((bf16[3072,4,288]{0,2,1:T(8,128)(2,1)}), bf16[3072,4,288]{0,2,1:T(8,128)(2,1)}, u32[]{:S(2)}, u32[]{:S(2)}) async-start(bf16[3072,4,288]{0,2,1:T(8,128)(2,1)} %bitcast.295), calls=%async_computation | async-start | bytes 14155776 | tf_op jit(solution)/shard_map/all_to_all | solution.py:16
  1148.6 218.5 %copy-start.23 = (bf16[144,96]{1,0:T(8,128)(2,1)S(1)}, bf16[144,96]{1,0:T(8,128)(2,1)}, u32[]{:S(2)}) copy-start(bf16[144,96]{1,0:T(8,128)(2,1)} %param.21) | copy-start | bytes 82948
  1148.6 474.7 %reduce-scatter.41.cloned.1.call-start = ((), (), s32[]{:S(2)}) async-start(), calls=%async_computation.41 | async-start | bytes 1990656 | tf_op jit(solution)/shard_map/reduce_scatter | solution.py:310
  1287.6 371.2 %reduce-scatter.45.cloned.1.call-start = ((), (), s32[]{:S(2)}) async-start(), calls=%async_computation.43 | async-start | bytes 1990656 | tf_op jit(solution)/shard_map/reduce_scatter | solution.py:313
  (20 other events, 111.6 us)
Sparse Core Ops, SparseCore 0:
  9.6 29.7 all-gather.24
  41.1 26.9 all-gather.28
  69.7 32.0 all-gather.40
  103.3 25.7 all-gather.36
  131.4 30.1 all-gather.18
  163.8 30.8 all-gather.20
  196.3 26.4 all-gather.34
  225.2 96.5 all-gather.16
  323.7 50.6 all-gather.22
  376.1 76.5 all-gather.26
  454.6 76.5 all-gather.30
  532.9 76.5 all-gather.42
  611.4 76.5 all-gather.38
  689.7 39.7 all-gather.44
  818.0 31.1 reduce-scatter.26
  852.0 31.1 reduce-scatter.28
  886.0 26.8 reduce-scatter.32
  915.7 26.8 reduce-scatter.34
  945.6 39.8 reduce-scatter.30
  988.3 39.8 reduce-scatter.36
  1031.2 76.5 reduce-scatter.46
  1109.4 26.4 all-gather.32
  1138.9 148.5 reduce-scatter.38
  1290.4 76.5 reduce-scatter.42
  1369.4 48.7 all-gather.46
  1420.9 30.9 reduce-scatter.50
  1454.6 29.0 reduce-scatter.52
  1486.0 30.3 reduce-scatter.48
  1518.7 30.3 reduce-scatter.54
  1551.3 35.2 reduce-scatter.56
  1589.0 34.2 reduce-scatter.40
  1625.6 33.1 reduce-scatter.44
